TPU v7x, 256 devices: a whole 4x4x8 slice. The times are simulated.
256 devices in a mesh: prompt: 16 (over z, core), comp: 16 (over x, y).
Axes of the slice: x: 4, y: 4, z: 8, core: 2. Of those that a mesh axis runs over, the one named last changes fastest.
Arguments:
- prompt_inner: bfloat16 [4096, 16384], P('prompt', 'comp'), may hold values from -0.59765625 to 0.59765625
- prompt_proj: bfloat16 [4096, 4096], P('prompt'), may hold values from -0.8984375 to 0.8984375
- prompt_step: float32 [256, 4096], P('comp', 'prompt')
- completion_inner: bfloat16 [32, 256, 16384], P('comp', None, 'prompt'), may hold values from -0.59765625 to 0.59765625
- completion_gate: bfloat16 [32, 256, 16384], P('comp', None, 'prompt'), may hold values from -12 to 12
- completion_projections: bfloat16 [32, 256, 4096], P('comp'), may hold values from -0.8984375 to 0.8984375
- sample_step: float32 [256, 32, 256], P('prompt', 'comp')
- sample_length: int32 [32], P('comp'), may hold values from 1 to 256, as said below
- decay_log: float32 [256], replicated
- conv_inner: bfloat16 [4, 16384], replicated, may hold values from -3 to 3
- conv_proj: bfloat16 [4, 4096], replicated, may hold values from -3 to 3
- norm_gain: float32 [16384], P('prompt'), may hold values from 0.5 to 1.5
Outputs:
- sample_out: bfloat16 [32, 256, 16384], P('comp', None, 'prompt')
Inputs may be any that keep to these rules, and one draw needn't show every extreme that they name: `sample_length`: some completion slot is full.
All inputs are finite; a program needn't handle non-finite values.
Results may differ from a plain program's by a relative error of at most 0.014.
Values may be sent and summed in bfloat16 or wider, within the bound.
A program may use at most 128 MiB of HBM per device.

v0:
```python
import jax
import jax.numpy as jnp
from jax import lax
from jax.sharding import PartitionSpec as P

STATE_HEADS = 256
HEAD_WIDTH = 64
STATE_WIDTH = 256
STATE_GROUPS = 8
CONV = 4
BLOCK = 128
EPS = 1e-05
HIGHEST = lax.Precision.HIGHEST


def from_behind(block, axis, distance):
    devices = range(lax.axis_size(axis))
    route = [(i - distance, i) for i in devices if i - distance in devices]
    return lax.ppermute(block, axis, route)


def carried_in(array, axis, combine, identity):
    peers, position = (lax.axis_size(axis), lax.axis_index(axis))
    everything = jax.tree.map(
        lambda part, kind: lax.all_gather(part.astype(kind), axis),
        array,
        (jnp.bfloat16, jnp.bfloat16),
    )
    start = jax.tree.map(
        lambda part, zero: jnp.broadcast_to(jnp.asarray(zero, part.dtype), part.shape),
        array,
        identity,
    )

    def hop(k, before):
        reached = k < position
        new = combine(
            before, jax.tree.map(lambda part, own: part[k].astype(own.dtype), everything, array)
        )
        return jax.tree.map(lambda a, b: jnp.where(reached, a, b), new, before)

    return lax.fori_loop(0, peers, hop, start)


def from_root(array, axis, root):
    mine = lax.axis_index(axis) == root
    return lax.psum(jnp.where(mine, array, jnp.zeros_like(array)), axis)


def from_partner(block, axis, stride):
    count = lax.axis_size(axis)
    route = []
    for low in range(count):
        high = low | 1 << stride
        if high != low and high < count:
            route += [(low, high), (high, low)]
    return lax.ppermute(block, axis, route)


def causal_conv(source, kernel, leading):
    padded = jnp.concatenate([leading, source], axis=0).astype(jnp.float32)
    kernel_wide = kernel.astype(jnp.float32)
    row_count = source.shape[0]
    summed = jnp.zeros(source.shape, jnp.float32)
    for offset in range(kernel.shape[0]):
        summed = summed + kernel_wide[offset] * padded[offset : offset + row_count]
    return jax.nn.silu(summed).astype(jnp.bfloat16)


def block_scan(state_in, inner_blk, b_blk, c_blk, step_blk, rate_vals):
    cumul = jnp.cumsum(-rate_vals[:, :, None] * step_blk, axis=2)
    scores = jnp.einsum("ign,jgn->gij", c_blk, b_blk, preferred_element_type=jnp.float32)
    spread_log = cumul[:, :, :, None] - cumul[:, :, None, :]
    length_q = step_blk.shape[2]
    causal = jnp.arange(length_q)[:, None] >= jnp.arange(length_q)[None, :]
    decay_mat = jnp.exp(jnp.where(causal, spread_log, -jnp.inf))
    mixer_w = (scores[:, None] * decay_mat * step_blk[:, :, None, :]).astype(jnp.bfloat16)
    intra_part = jnp.einsum(
        "gkij,jgkd->igkd", mixer_w, inner_blk, preferred_element_type=jnp.float32
    )
    readout = jnp.einsum("ign,gkdn->igkd", c_blk.astype(jnp.float32), state_in, precision=HIGHEST)
    inter_part = jnp.transpose(jnp.exp(cumul), (2, 0, 1))[..., None] * readout
    weights = jnp.exp(cumul[:, :, -1:] - cumul) * step_blk
    packed = (inner_blk.astype(jnp.float32) * jnp.transpose(weights, (2, 0, 1))[..., None]).astype(
        jnp.bfloat16
    )
    fresh_part = jnp.einsum("jgn,jgkd->gkdn", b_blk, packed, preferred_element_type=jnp.float32)
    return (
        intra_part + inter_part,
        jnp.exp(cumul[:, :, -1])[..., None, None] * state_in + fresh_part,
    )


def local(
    prompt_inner,
    prompt_proj,
    prompt_step,
    completion_inner,
    completion_gate,
    completion_projections,
    sample_step,
    sample_length,
    decay_log,
    conv_inner,
    conv_proj,
    norm_gain,
):
    prompt_count = lax.axis_size("prompt")
    prompt_idx = lax.axis_index("prompt")
    column_idx = lax.axis_index("comp")
    heads_group = STATE_HEADS // STATE_GROUPS
    heads_col = prompt_step.shape[0]
    heads_row = sample_step.shape[0]
    state_feats = STATE_GROUPS * STATE_WIDTH
    lag_rows = CONV - 1
    rows_prompt = prompt_inner.shape[0]
    prev_inner, prev_proj = from_behind(
        (
            prompt_inner[rows_prompt - lag_rows :],
            prompt_proj[rows_prompt - lag_rows :, :state_feats],
        ),
        "prompt",
        1,
    )
    col_start = column_idx * heads_col
    conv_col = lax.dynamic_slice_in_dim(
        conv_inner, col_start * HEAD_WIDTH, heads_col * HEAD_WIDTH, 1
    )
    inner_conv = causal_conv(prompt_inner, conv_col, prev_inner)
    b_conv = causal_conv(prompt_proj[:, :state_feats], conv_proj[:, :state_feats], prev_proj)
    rate_col = jnp.exp(lax.dynamic_slice_in_dim(decay_log, col_start, heads_col, 0))
    step_col = jax.nn.softplus(prompt_step)
    cumul = jnp.cumsum(-rate_col[:, None] * step_col, axis=1)
    local_log = cumul[:, -1]
    weight_col = jnp.exp(local_log[:, None] - cumul) * step_col
    group_span = max(1, heads_col // heads_group)
    per_group = heads_col // group_span
    group_start = col_start // heads_group
    b_select = lax.dynamic_slice_in_dim(
        b_conv.reshape(rows_prompt, STATE_GROUPS, STATE_WIDTH), group_start, group_span, 1
    ).astype(jnp.float32)
    scaled = (
        inner_conv.astype(jnp.float32).reshape(rows_prompt, heads_col, HEAD_WIDTH)
        * jnp.transpose(weight_col)[:, :, None]
    )
    scaled = scaled.reshape(rows_prompt, group_span, per_group, HEAD_WIDTH)
    local_state = jnp.einsum("tgn,tghd->ghdn", b_select, scaled, precision=HIGHEST).reshape(
        heads_col, HEAD_WIDTH, STATE_WIDTH
    )
    own_inner = prompt_inner[rows_prompt - lag_rows :].astype(jnp.float32)
    own_proj = prompt_proj[rows_prompt - lag_rows :].astype(jnp.float32)
    last_index = prompt_count - 1
    head_start = prompt_idx * heads_row
    owner = head_start // heads_col

    def combine(earlier, later):
        return (earlier[0] + later[0], earlier[1] * jnp.exp(later[0])[:, None, None] + later[1])

    before = carried_in(
        (local_log, local_state),
        "prompt",
        combine,
        (jnp.zeros_like(local_log), jnp.zeros_like(local_state)),
    )
    through = combine(before, (local_log, local_state))[1]
    final_state, tail_inner, tail_proj = (
        from_root(through.astype(jnp.bfloat16), "prompt", last_index).astype(through.dtype),
        from_root(own_inner.astype(jnp.bfloat16), "prompt", last_index).astype(own_inner.dtype),
        from_root(own_proj.astype(jnp.bfloat16), "prompt", last_index).astype(own_proj.dtype),
    )
    moved_state, moved_inner = (
        from_root(final_state.astype(jnp.bfloat16), "comp", owner).astype(final_state.dtype),
        from_root(tail_inner.astype(jnp.bfloat16), "comp", owner).astype(tail_inner.dtype),
    )
    lead_inner = moved_inner.astype(jnp.bfloat16)
    group_row = head_start // heads_group
    b_start = group_row * STATE_WIDTH
    c_start = state_feats + group_row * STATE_WIDTH
    proj_select = jnp.concatenate(
        [
            lax.dynamic_slice_in_dim(completion_projections, b_start, STATE_WIDTH, 2),
            lax.dynamic_slice_in_dim(completion_projections, c_start, STATE_WIDTH, 2),
        ],
        axis=2,
    )
    kernel_select = jnp.concatenate(
        [
            lax.dynamic_slice_in_dim(conv_proj, b_start, STATE_WIDTH, 1),
            lax.dynamic_slice_in_dim(conv_proj, c_start, STATE_WIDTH, 1),
        ],
        axis=1,
    )
    lead_wide = tail_proj.astype(jnp.bfloat16)
    lead_select = jnp.concatenate(
        [
            lax.dynamic_slice_in_dim(lead_wide, b_start, STATE_WIDTH, 1),
            lax.dynamic_slice_in_dim(lead_wide, c_start, STATE_WIDTH, 1),
        ],
        axis=1,
    )
    conv_row = lax.dynamic_slice_in_dim(
        conv_inner, head_start * HEAD_WIDTH, heads_row * HEAD_WIDTH, 1
    )
    rate_row = jnp.exp(lax.dynamic_slice_in_dim(decay_log, head_start, heads_row, 0))
    step_row = jax.nn.softplus(sample_step)
    slot_count = completion_inner.shape[0]
    sample_len = completion_inner.shape[1]
    block_count = sample_len // BLOCK

    def advance(carry, block_in):
        block_out, carry_next = block_scan(
            carry, block_in[0], block_in[1], block_in[2], block_in[3], rate_row[None]
        )
        return (carry_next, block_out)

    gated_list = []
    square_list = []
    for slot in range(slot_count):
        slot_conv = causal_conv(completion_inner[slot], conv_row, lead_inner)
        proj_conv = causal_conv(proj_select[slot], kernel_select, lead_select)
        inner_blocks = slot_conv.reshape(block_count, BLOCK, 1, heads_row, HEAD_WIDTH)
        b_blocks = proj_conv[:, :STATE_WIDTH].reshape(block_count, BLOCK, 1, STATE_WIDTH)
        c_blocks = proj_conv[:, STATE_WIDTH:].reshape(block_count, BLOCK, 1, STATE_WIDTH)
        step_blocks = jnp.transpose(
            step_row[:, slot].reshape(heads_row, block_count, BLOCK), (1, 0, 2)
        )[:, None]
        block_inputs = (inner_blocks, b_blocks, c_blocks, step_blocks)
        _, block_outs = lax.scan(advance, moved_state[None], block_inputs)
        ssm_out = block_outs.reshape(sample_len, heads_row * HEAD_WIDTH)
        gated = ssm_out * jax.nn.silu(completion_gate[slot].astype(jnp.float32))
        gated_list.append(gated)
        square_list.append(jnp.sum(gated * gated, axis=1))
    square_all = jnp.stack(square_list)
    square_all = square_all + from_partner(square_all, "prompt", 0)
    scale_all = lax.rsqrt(square_all / (heads_group * HEAD_WIDTH) + EPS)
    gated_all = jnp.stack(gated_list)
    result = gated_all * scale_all[:, :, None] * norm_gain[None, None, :]
    live_rows = jnp.arange(sample_len)[None, :] < sample_length[:, None]
    return jnp.where(live_rows[:, :, None], result, 0.0).astype(jnp.bfloat16)


def solution(mesh):
    placed = (
        P("prompt", "comp"),
        P("prompt", None),
        P("comp", "prompt"),
        P("comp", None, "prompt"),
        P("comp", None, "prompt"),
        P("comp", None, None),
        P("prompt", "comp", None),
        P("comp"),
        P(),
        P(),
        P(),
        P("prompt"),
    )
    return jax.shard_map(
        local, mesh=mesh, in_specs=placed, out_specs=P("comp", None, "prompt"), check_vma=False
    )
```

profile of v0, /device:TPU:1, one launch (start us, length us, event | category | flops | bytes accessed | tf_op | source)
XLA Modules:
  0.0 410.7 jit_solution(14466374462376283287)
XLA Ops:
  7.3 4.9 %collective-permute-start = (bf16[3,1024]{1,0:T(4,128)(2,1)S(1)}, bf16[3,1024]{1,0:T(4,128)(2,1)S(1)}, u32[]{:S(2)}, u32[]{:S(2)}) collective-permute-start(bf16[3,1024]{1,0:T(4,128)(2,1)S(1)} %get-tuple-element.414), channel_id=1, source_target_pairs={{0,16},{16,32},{32,48},{48,64},{64,80},{80,96},{96,112},{112,128},... | collective-permute-start | bytes 18440 | tf_op jit(solution)/shard_map/ppermute | solution.py:19
  13.0 1.9 collective-permute-start.1
  14.9 1.3 negate_bitcast_fusion
  20.4 1.2 copy.68
  22.2 1.6 bitcast_multiply_fusion
  24.2 1.3 multiply_convert_fusion.6
  26.1 1.4 fusion.107
  29.3 0.9 slice_select_fusion
  30.2 46.1 %all-reduce.1 = (bf16[256]{0:T(256)(128)(2,1)S(1)}, bf16[3,1024]{1,0:T(4,128)(2,1)S(1)}, bf16[3,4096]{1,0:T(4,128)(2,1)S(1)}) all-reduce(bf16[256]{0:T(256)(128)(2,1)S(1)} %dynamic-update-slice, bf16[3,1024]{1,0:T(4,128)(2,1)S(1)} %get-tuple-element.413, ...), channel_id=2, replica_groups=mesh['prompt'=16,'comp'=16] {'prompt'}, use_global_device_ids=true, to_apply=%add | all-reduce | flops 15616 | bytes 62464
  76.4 35.3 %psum.38 = bf16[3,1024]{1,0:T(4,128)(2,1)S(1)} all-reduce(bf16[3,1024]{1,0:T(4,128)(2,1)S(1)} %broadcast_select_fusion.1), channel_id=1, replica_groups=mesh['prompt'=16,'comp'=16] {'comp'}, use_global_device_ids=true, to_apply=%region_7.8 | all-reduce | flops 3072 | bytes 12288 | tf_op jit(solution)/shard_map/psum | solution.py:47
  111.9 2.1 fusion.99
  114.2 1.2 copy.92
  116.2 1.1 constant_dynamic-slice_fusion.3
  118.4 1.4 multiply_convert_fusion.11
  119.7 2.4 multiply_convert_fusion.8
  122.1 21.4 %while.44 = (s32[]{:T(128)}, f32[16,64,256]{2,1,0:T(8,128)S(1)}, s32[]{:T(128)}, bf16[16,16]{1,0:T(8,128)(2,1)S(1)}, bf16[16,16,64,256]{3,2,1,0:T(8,128)(2,1)}, /*index=5*/s32[]{:T(128)}, s32[]{:T(128)}) while((s32[]{:T(128)}, f32[16,64,256]{2,1,0:T(8,128)S(1)}, s32[]{:T(128)}, bf16[16,16]{1,0:T(8,128)(2,1)S(1)}, ...), condition=%wide.region_3.4_spmd.clone, body=%wide.region_2.3_spmd.clone.sunk | while | flops 1310740 | bytes 2621713 | solution.py:42
  122.2 1.3 fusion.154
  123.5 1.3 fusion.154
  124.9 1.3 fusion.154
  126.2 1.3 fusion.154
  127.6 1.3 fusion.154
  128.9 1.3 fusion.154
  130.2 1.3 fusion.154
  131.6 1.3 fusion.154
  132.9 1.3 fusion.154
  134.3 1.3 fusion.154
  135.6 1.3 fusion.154
  136.9 1.3 fusion.154
  138.3 1.3 fusion.154
  139.6 1.3 fusion.154
  141.0 1.3 fusion.154
  142.3 1.3 fusion.154
  143.6 1.0 fusion.84
  144.9 2.1 fusion.98
  146.9 114.7 %all-reduce.5.cloned.1.call-done = bf16[16,64,256]{2,1,0:T(8,128)(2,1)} async-done(((bf16[16,64,256]{2,1,0:T(8,128)(2,1)}), bf16[16,64,256]{2,1,0:T(8,128)(2,1)}) %all-reduce.5.cloned.1.call-update) | async-done | bytes 524304 | tf_op jit(solution)/shard_map/psum | solution.py:47
  263.2 0.9 copy.79
  264.1 0.8 copy.93
  265.1 1.0 copy.73
  266.1 0.8 copy.91
  267.0 2.1 convert_element_type.228
  269.0 2.1 convert_element_type.223
  272.4 87.0 %all-reduce.7.cloned.1.call-done = bf16[1,16,64,256]{3,2,1,0:T(8,128)(2,1)} async-done(((bf16[1,16,64,256]{3,2,1,0:T(8,128)(2,1)}), bf16[1,16,64,256]{3,2,1,0:T(8,128)(2,1)}) %all-reduce.7.cloned.1.call-update) | async-done | bytes 524304 | tf_op jit(solution)/shard_map/psum | solution.py:47
  359.5 1.1 broadcast_in_dim.90
  360.7 1.1 broadcast.247.clone
  361.8 16.0 %while.43 = (s32[]{:T(128)}, f32[1,16,64,256]{3,2,1,0:T(8,128)S(1)}, f32[2,128,1,16,64]{1,4,3,2,0:T(8,128)}, f32[1,16,1]{1,2,0:T(1,128)}, f32[2,1,16,128]{3,0,2,...) while((s32[]{:T(128)}, ...), condition=%wide.region_14.15_spmd, body=%wide.region_12.14_spmd.sunk | while | flops 514478080 | bytes 16805992 | solution.py:228
  362.5 1.2 broadcast_multiply_fusion.5
  363.8 1.0 reduce_window_sum.44
  365.0 1.6 fusion.151
  366.6 1.4 fusion.150
  368.8 1.0 copy-done.3
  370.5 1.2 broadcast_multiply_fusion.5
  371.8 1.0 reduce_window_sum.44
  373.0 1.6 fusion.151
  374.6 1.4 fusion.150
  376.8 1.0 copy-done.3
  377.8 2.1 copy.80
  379.9 3.0 fusion.72
  383.1 8.1 %while.42 = (s32[]{:T(128)}, f32[1,16,64,256]{3,2,1,0:T(8,128)S(1)}, f32[2,128,1,16,64]{1,4,3,2,0:T(8,128)S(1)}, f32[1,16,1]{1,2,0:T(1,128)}, f32[2,1,16,128]{3,...) while((s32[]{:T(128)}, ...), condition=%wide.region_11.12_spmd, body=%wide.region_9.11_spmd.sunk | while | flops 514478080 | bytes 7893013 | solution.py:228
  385.0 1.4 fusion.139
  389.0 1.4 fusion.139
  393.5 2.3 collective-permute-start.2
  395.8 2.2 fusion.71
  398.1 3.6 fusion.70
  401.7 2.5 copy.86
  (158 shorter events, 25.0 us)
Async XLA Ops:
  6.5 115.6 %all-gather.4.cloned.1.call-start = ((), (), s32[]{:S(2)}) async-start(), calls=%async_computation.2 | async-start | bytes 8912896 | tf_op jit(solution)/shard_map/all_gather | solution.py:25
  7.3 14.4 %collective-permute-start = (bf16[3,1024]{1,0:T(4,128)(2,1)S(1)}, bf16[3,1024]{1,0:T(4,128)(2,1)S(1)}, u32[]{:S(2)}, u32[]{:S(2)}) collective-permute-start(bf16[3,1024]{1,0:T(4,128)(2,1)S(1)} %get-tuple-element.414), channel_id=1, source_target_pairs={{0,16},{16,32},{32,48},{48,64},{64,80},{80,96},{96,112},{112,128},... | collective-permute-start | bytes 18440 | tf_op jit(solution)/shard_map/ppermute | solution.py:19
  13.0 10.9 %collective-permute-start.1 = (bf16[3,2048]{1,0:T(4,128)(2,1)S(1)}, bf16[3,2048]{1,0:T(4,128)(2,1)S(1)}, u32[]{:S(2)}, u32[]{:S(2)}) collective-permute-start(bf16[3,2048]{1,0:T(4,128)(2,1)S(1)} %slice.215), channel_id=1, source_target_pairs={{0,16},{16,32},{32,48},{48,64},{64,80},{80,96},{96,112},{112,128},... | collective-permute-start | bytes 36872 | tf_op jit(solution)/shard_map/ppermute | solution.py:19
  22.2 1.6 slice-start
  25.8 1.8 copy-start.18
  27.5 234.1 %all-reduce.5.cloned.1.call-start = ((), (), s32[]{:S(2)}) async-start(), calls=%async_computation | async-start | bytes 1048576 | tf_op jit(solution)/shard_map/psum | solution.py:47
  117.5 0.8 copy-start.14
  144.6 117.8 %copy-start.17 = (s32[2]{0:T(128)S(1)}, s32[2]{0:T(128)}, u32[]{:S(2)}) copy-start(s32[2]{0:T(128)} %param.25) | copy-start | bytes 28
  144.6 214.8 %all-reduce.7.cloned.1.call-start = ((), (), s32[]{:S(2)}) async-start(), calls=%async_computation.1 | async-start | bytes 1048576 | tf_op jit(solution)/shard_map/psum | solution.py:47
  264.1 2.0 copy-start.11
  264.9 4.1 copy-start
  267.0 4.8 %copy-start.12 = (bf16[256,512]{1,0:T(8,128)(2,1)S(1)}, bf16[256,512]{1,0:T(8,128)(2,1)}, u32[]{:S(2)}) copy-start(bf16[256,512]{1,0:T(8,128)(2,1)} %get-tuple-element.444) | copy-start | bytes 786436
  364.7 3.3 copy-start.7
  365.0 3.2 copy-start.2
  365.0 3.3 copy-start.6
  368.8 1.0 copy-start.3
  372.7 3.3 copy-start.7
  373.0 3.2 copy-start.2
  373.0 3.2 copy-start.6
  376.8 1.0 copy-start.3
  377.8 2.1 copy-start.1
  379.9 3.2 copy-start.13
  384.3 2.3 copy-start.5
  388.4 2.3 copy-start.5
  391.2 1.2 copy-start.4
  391.2 1.5 copy-start.10
  391.2 1.9 copy-start.9
  393.5 4.6 %copy-start.8 = (f32[1,256,1024]{1,0,2:T(1,128)S(1)}, f32[1,256,1024]{1,0,2:T(1,128)}, u32[]{:S(2)}) copy-start(f32[1,256,1024]{1,0,2:T(1,128)} %fusion.72) | copy-start | bytes 3145732
  393.5 4.6 %copy-start.15 = (f32[1024]{0:T(1024)S(1)}, f32[1024]{0:T(1024)}, u32[]{:S(2)}) copy-start(f32[1024]{0:T(1024)} %param.29) | copy-start | bytes 12292
  393.5 4.6 %copy-start.16 = (pred[2,256]{1,0:T(4,128)(4,1)S(1)}, pred[2,256]{1,0:T(4,128)(4,1)}, u32[]{:S(2)}) copy-start(pred[2,256]{1,0:T(4,128)(4,1)} %iota_compare_fusion.2) | copy-start | bytes 1540
  393.5 4.5 %collective-permute-start.2 = (f32[2,256]{1,0:T(2,128)S(1)}, f32[2,256]{1,0:T(2,128)S(1)}, u32[]{:S(2)}, u32[]{:S(2)}) collective-permute-start(f32[2,256]{1,0:T(2,128)S(1)} %pad_maximum_fusion.4), channel_id=1, source_target_pairs={{0,16},{16,0},{32,48},{48,32},{64,80},{80,64},{96,112},{112,96},{1... | collective-permute-start | bytes 6152 | tf_op jit(solution)/shard_map/ppermute | solution.py:57
Sparse Core Ops, SparseCore 0:
  27.6 58.7 all-gather.3
  144.7 116.7 all-reduce.4
  265.1 94.3 all-reduce.6
where the time goes:
time: 413 us; the launch traced here: 411 us
  waiting for transfers between devices  202 us (49%)
  blocking collectives  81.4 us (20%)
  other arithmetic  59.8 us (14%)
  local copies, waits for them, and re-layouts  29 us (7%)
  between operations  14.3 us (3%)
  matrix products  14.2 us (3%)
  starting transfers between devices  9.41 us (2%)
    psum x2, waiting for transfers between devices, from_root(): return lax.psum(jnp.where(mine, array, jnp.zeros_like(array)), axis)  202 us
    unnamed x1, blocking collectives  46.1 us
    psum x1, blocking collectives, from_root(): return lax.psum(jnp.where(mine, array, jnp.zeros_like(array)), axis)  35.3 us
    select_n x16, other arithmetic, hop(): return jax.tree.map(lambda a, b: jnp.where(reached, a, b), new, before)  20.7 us
  transfers between devices with their start and end apart: 6, of which 2 were waited for; matrix products, arithmetic and copies ran while one was open for 9% of the time, Pallas kernels for 0%

commit v1 on v0

--- a/solution.py
+++ b/solution.py
@@ -44,7 +44,7 @@
 
 def from_root(array, axis, root):
     mine = lax.axis_index(axis) == root
-    return lax.psum(jnp.where(mine, array, jnp.zeros_like(array)), axis)
+    return jnp.sum(lax.all_gather(jnp.where(mine, array, jnp.zeros_like(array)), axis), axis=0)
 
 
 def from_partner(block, axis, stride):

time: 413 us -> 302 us (0.73)
  waiting for transfers between devices: 202 us -> 85.9 us
  other arithmetic: 59.8 us -> 68.8 us
    psum x2 -> x0, waiting for transfers between devices: 202 us -> none  [from_root(): return lax.psum(jnp.where(mine, array, jnp.zeros_like(array)), axis)]
    all_gather x0 -> x3, blocking collectives: none -> 55.8 us  [from_root(): lax.all_gather(jnp.where(mine, array, jnp.zeros_like(array)), axis)]
    all_gather x0 -> x2, waiting for transfers between devices: none -> 54.5 us  [from_root(): lax.all_gather(jnp.where(mine, array, jnp.zeros_like(array)), axis)]
    psum x1 -> x0, blocking collectives: 35.3 us -> none  [from_root(): return lax.psum(jnp.where(mine, array, jnp.zeros_like(array)), axis)]
    all_gather x1, waiting for transfers between devices: 0.02 us -> 31.3 us  [carried_in(): lax.all_gather(part.astype(kind), axis)]
    unnamed x1, blocking collectives: 46.1 us -> 25.3 us
    reduce_sum x0 -> x5, other arithmetic: none -> 10.9 us  [from_root(): jnp.sum(lax.all_gather(jnp.where(mine, array, jnp.zeros_like(array)), axi...]
  transfers between devices with their start and end apart: 6 -> 6, of which waited for: 2 -> 2; matrix products, arithmetic and copies ran while one was open for 9% -> 11% of each run, Pallas kernels for 0% -> 0%
where the time goes in v1:
time: 302 us; the launch traced here: 300 us
  waiting for transfers between devices  85.9 us (28%)
  blocking collectives  81.1 us (27%)
  other arithmetic  68.8 us (23%)
  local copies, waits for them, and re-layouts  27.1 us (9%)
  between operations  14.3 us (5%)
  matrix products  14.2 us (5%)
  starting transfers between devices  7.16 us (2%)
    all_gather x3, blocking collectives, from_root(): lax.all_gather(jnp.where(mine, array, jnp.zeros_like(array)), axis)  55.8 us
    all_gather x2, waiting for transfers between devices, from_root(): lax.all_gather(jnp.where(mine, array, jnp.zeros_like(array)), axis)  54.5 us
    all_gather x1, waiting for transfers between devices, carried_in(): lax.all_gather(part.astype(kind), axis)  31.3 us
    unnamed x1, blocking collectives  25.3 us
    select_n x16, other arithmetic, hop(): return jax.tree.map(lambda a, b: jnp.where(reached, a, b), new, before)  20.7 us
    reduce_sum x5, other arithmetic, from_root(): jnp.sum(lax.all_gather(jnp.where(mine, array, jnp.zeros_like(array)), axi...  10.9 us
    ppermute x2, starting transfers between devices, from_behind(): return lax.ppermute(block, axis, route)  6.86 us
  transfers between devices with their start and end apart: 6, of which 2 were waited for; matrix products, arithmetic and copies ran while one was open for 11% of the time, Pallas kernels for 0%

profile of v1, /device:TPU:1, one launch (start us, length us, event | category | flops | bytes accessed | tf_op | source)
XLA Modules:
  0.0 299.6 jit_solution(12301456681415351991)
XLA Ops:
  7.3 4.9 %collective-permute-start = (bf16[3,1024]{1,0:T(4,128)(2,1)S(1)}, bf16[3,1024]{1,0:T(4,128)(2,1)S(1)}, u32[]{:S(2)}, u32[]{:S(2)}) collective-permute-start(bf16[3,1024]{1,0:T(4,128)(2,1)S(1)} %get-tuple-element.427), channel_id=1, source_target_pairs={{0,16},{16,32},{32,48},{48,64},{64,80},{80,96},{96,112},{112,128},... | collective-permute-start | bytes 18440 | tf_op jit(solution)/shard_map/ppermute | solution.py:19
  13.0 1.9 collective-permute-start.1
  14.9 1.4 negate_bitcast_fusion
  20.5 1.2 copy.84
  22.4 1.6 bitcast_multiply_fusion
  24.3 1.3 multiply_convert_fusion.6
  26.2 1.4 fusion.107
  29.4 25.3 %all-reduce = bf16[256]{0:T(256)(128)(2,1)S(1)} all-reduce(bf16[256]{0:T(256)(128)(2,1)S(1)} %dynamic-update-slice), channel_id=2, replica_groups=mesh['prompt'=16,'comp'=16] {'prompt'}, use_global_device_ids=true, to_apply=%add | all-reduce | flops 256 | bytes 1024
  54.8 31.3 %all-gather.14.cloned.1.call-done = bf16[256,64,256]{2,1,0:T(8,128)(2,1)} async-done(((bf16[16,64,256]{2,1,0:T(8,128)(2,1)}), bf16[256,64,256]{2,1,0:T(8,128)(2,1)}) %all-gather.14.cloned.1.call-update) | async-done | bytes 8388624 | tf_op jit(solution)/shard_map/all_gather | solution.py:25
  86.1 21.4 %while.44 = (s32[]{:T(128)}, f32[16,64,256]{2,1,0:T(8,128)S(1)}, s32[]{:T(128)}, bf16[16,16]{1,0:T(8,128)(2,1)S(1)}, bf16[16,16,64,256]{3,2,1,0:T(8,128)(2,1)}, /*index=5*/s32[]{:T(128)}, s32[]{:T(128)}) while((s32[]{:T(128)}, f32[16,64,256]{2,1,0:T(8,128)S(1)}, s32[]{:T(128)}, bf16[16,16]{1,0:T(8,128)(2,1)S(1)}, ...), condition=%wide.region_3.4_spmd.clone, body=%wide.region_2.3_spmd.clone.sunk | while | flops 1310740 | bytes 2621713 | solution.py:42
  86.2 1.3 fusion.154
  87.5 1.3 fusion.154
  88.8 1.3 fusion.154
  90.2 1.3 fusion.154
  91.5 1.3 fusion.154
  92.9 1.3 fusion.154
  94.2 1.3 fusion.154
  95.5 1.3 fusion.154
  96.9 1.3 fusion.154
  98.2 1.3 fusion.154
  99.6 1.3 fusion.154
  100.9 1.3 fusion.154
  102.2 1.3 fusion.154
  103.6 1.3 fusion.154
  104.9 1.3 fusion.154
  106.3 1.3 fusion.154
  107.6 1.0 fusion.84
  108.7 54.5 %all-gather.16.cloned.1.call-done = bf16[256,64,256]{2,1,0:T(8,128)(2,1)} async-done(((bf16[16,64,256]{2,1,0:T(8,128)(2,1)}), bf16[256,64,256]{2,1,0:T(8,128)(2,1)}) %all-gather.16.cloned.1.call-update) | async-done | bytes 8388624 | tf_op jit(solution)/shard_map/all_gather | solution.py:47
  163.2 5.3 %reduce_sum.78 = bf16[16,64,256]{2,1,0:T(8,128)(2,1)S(1)} reduce(bf16[16,16,64,256]{3,2,1,0:T(8,128)(2,1)} %bitcast.290, bf16[]{:T(256)} %constant.169.clone.1), dimensions={0}, to_apply=%region_4.5 | reduce | flops 3932160 | bytes 8912898 | tf_op jit(solution)/shard_map/reduce_sum | solution.py:47
  168.5 0.8 broadcast_select_fusion
  169.3 15.9 %all-gather.7 = bf16[16,3,1024]{2,1,0:T(4,128)(2,1)S(1)} all-gather(bf16[1,3,1024]{2,1,0:T(4,128)(2,1)S(1)} %get-tuple-element.426), channel_id=6, replica_groups=mesh['prompt'=16,'comp'=16] {'prompt'}, dimensions={0}, use_global_device_ids=true | all-gather | bytes 104448 | tf_op jit(solution)/shard_map/all_gather | solution.py:47
  185.3 19.0 %all-gather.8 = bf16[16,3,1024]{2,1,0:T(4,128)(2,1)S(1)} all-gather(bf16[1,3,1024]{2,1,0:T(4,128)(2,1)S(1)} %select_bitcast_fusion.1), channel_id=7, replica_groups=mesh['prompt'=16,'comp'=16] {'comp'}, dimensions={0}, use_global_device_ids=true | all-gather | bytes 104448 | tf_op jit(solution)/shard_map/all_gather | solution.py:47
  205.8 2.4 multiply_convert_fusion.8
  208.2 1.0 reshape.632
  209.2 2.0 copy.95
  211.2 20.8 %all-gather.9 = bf16[16,3,4096]{2,1,0:T(4,128)(2,1)S(1)} all-gather(bf16[1,3,4096]{2,1,0:T(4,128)(2,1)S(1)} %select_bitcast_fusion), channel_id=8, replica_groups=mesh['prompt'=16,'comp'=16] {'prompt'}, dimensions={0}, use_global_device_ids=true | all-gather | bytes 417792 | tf_op jit(solution)/shard_map/all_gather | solution.py:47
  232.2 1.3 fusion.98
  233.5 1.0 copy.109
  234.7 1.0 copy.89
  235.7 0.8 copy.107
  236.6 2.1 convert_element_type.252
  238.7 2.0 convert_element_type.247
  241.5 1.1 constant_dynamic-slice_fusion.3
  245.5 5.3 %reduce_sum.79 = bf16[16,64,256]{2,1,0:T(8,128)(2,1)S(1)} reduce(bf16[16,16,64,256]{3,2,1,0:T(8,128)(2,1)} %bitcast.289, bf16[]{:T(256)} %constant.169.clone.1), dimensions={0}, to_apply=%region_5.6 | reduce | flops 3932160 | bytes 8912898 | tf_op jit(solution)/shard_map/reduce_sum | solution.py:47
  251.0 1.1 broadcast.283.clone
  252.1 16.2 %while.43 = (s32[]{:T(128)}, f32[1,16,64,256]{3,2,1,0:T(8,128)S(1)}, f32[2,128,1,16,64]{1,4,3,2,0:T(8,128)}, f32[1,16,1]{1,2,0:T(1,128)}, f32[2,1,16,128]{3,0,2,...) while((s32[]{:T(128)}, ...), condition=%wide.region_14.15_spmd, body=%wide.region_12.14_spmd.sunk | while | flops 514478080 | bytes 16805992 | solution.py:228
  252.8 1.4 broadcast_multiply_fusion.5
  254.2 1.0 reduce_window_sum.44
  255.4 1.6 fusion.151
  257.0 1.4 fusion.150
  259.2 1.0 copy-done.3
  260.9 1.4 broadcast_multiply_fusion.5
  262.3 1.0 reduce_window_sum.44
  263.5 1.6 fusion.151
  265.1 1.4 fusion.150
  267.4 1.0 copy-done.3
  268.3 2.1 copy.96
  270.5 3.0 %fusion.72 = f32[1,256,1024]{1,0,2:T(1,128)} fusion(f32[1,256,1024]{1,0,2:T(1,128)S(1)} %bitcast.298, bf16[1,256,1024]{1,0,2:T(2,128)(2,1)S(1)} %copy-done.1), kind=kLoop, calls=%fused_computation.103 | loop fusion | flops 1572864 | bytes 2621440 | tf_op jit(solution)/shard_map/mul | solution.py:230
  273.6 8.6 %while.42 = (s32[]{:T(128)}, f32[1,16,64,256]{3,2,1,0:T(8,128)S(1)}, f32[2,128,1,16,64]{1,4,3,2,0:T(8,128)S(1)}, f32[1,16,1]{1,2,0:T(1,128)}, f32[2,1,16,128]{3,...) while((s32[]{:T(128)}, ...), condition=%wide.region_11.12_spmd, body=%wide.region_9.11_spmd.sunk | while | flops 514478080 | bytes 7893013 | solution.py:228
  275.6 1.4 fusion.139
  279.8 1.4 fusion.139
  284.7 2.2 fusion.71
  287.0 3.6 %fusion.70 = bf16[2,256,1024]{1,0,2:T(2,128)(2,1)S(1)} fusion(f32[1,256,1024]{1,0,2:T(1,128)S(1)} %copy-done.8, f32[1,256,1024]{1,0,2:T(1,128)S(1)} %fusion.71, pred[2,256]{1,0:T(4,128)(4,1)S(1)} %copy-done.16, f32[1024]{0:T(1024)S(1)} %copy-done.15, f32[2,256]{1,0:T(2,128)S(1)} %add_rsqrt_fusion), kind=kLoop, calls=%fused_computation.98 | loop fusion | flops 2621440 | bytes 3152384 | tf_op jit(solution)/shard_map/convert_element_type | solution.py:239
  290.6 2.5 copy.102
  (165 shorter events, 25.7 us)
Async XLA Ops:
  6.5 79.6 %all-gather.14.cloned.1.call-start = ((), (), s32[]{:S(2)}) async-start(), calls=%async_computation | async-start | bytes 8912896 | tf_op jit(solution)/shard_map/all_gather | solution.py:25
  7.3 14.5 %collective-permute-start = (bf16[3,1024]{1,0:T(4,128)(2,1)S(1)}, bf16[3,1024]{1,0:T(4,128)(2,1)S(1)}, u32[]{:S(2)}, u32[]{:S(2)}) collective-permute-start(bf16[3,1024]{1,0:T(4,128)(2,1)S(1)} %get-tuple-element.427), channel_id=1, source_target_pairs={{0,16},{16,32},{32,48},{48,64},{64,80},{80,96},{96,112},{112,128},... | collective-permute-start | bytes 18440 | tf_op jit(solution)/shard_map/ppermute | solution.py:19
  13.0 11.0 %collective-permute-start.1 = (bf16[3,2048]{1,0:T(4,128)(2,1)S(1)}, bf16[3,2048]{1,0:T(4,128)(2,1)S(1)}, u32[]{:S(2)}, u32[]{:S(2)}) collective-permute-start(bf16[3,2048]{1,0:T(4,128)(2,1)S(1)} %slice.215), channel_id=1, source_target_pairs={{0,16},{16,32},{32,48},{48,64},{64,80},{80,96},{96,112},{112,128},... | collective-permute-start | bytes 36872 | tf_op jit(solution)/shard_map/ppermute | solution.py:19
  22.3 1.6 slice-start
  25.9 1.8 copy-start.18
  27.6 135.6 %all-gather.16.cloned.1.call-start = ((), (), s32[]{:S(2)}) async-start(), calls=%async_computation.1 | async-start | bytes 8912896 | tf_op jit(solution)/shard_map/all_gather | solution.py:47
  108.6 136.9 %all-gather.18.cloned.1.call-start = ((), (), s32[]{:S(2)}) async-start(), calls=%async_computation.2 | async-start | bytes 8912896 | tf_op jit(solution)/shard_map/all_gather | solution.py:47
  168.5 36.2 %copy-start.12 = (bf16[2,256,1024]{2,1,0:T(8,128)(2,1)S(1)}, bf16[2,256,1024]{2,1,0:T(8,128)(2,1)}, u32[]{:S(2)}) copy-start(bf16[2,256,1024]{2,1,0:T(8,128)(2,1)} %param.21) | copy-start | bytes 3145732
  208.2 2.9 copy-start.9
  234.6 4.1 %copy-start = (bf16[1,256,1024]{1,0,2:T(2,128)(2,1)}, bf16[1,256,1024]{1,0,2:T(2,128)(2,1)S(1)}, u32[]{:S(2)}) copy-start(bf16[1,256,1024]{1,0,2:T(2,128)(2,1)S(1)} %copy.109) | copy-start | bytes 1572868
  240.7 2.0 copy-start.17
  240.8 2.7 copy-start.14
  255.2 3.3 %copy-start.7 = (bf16[2,128,1,256]{3,1,2,0:T(8,128)(2,1)S(1)}, bf16[2,128,1,256]{3,1,2,0:T(8,128)(2,1)}, u32[]{:S(2)}) copy-start(bf16[2,128,1,256]{3,1,2,0:T(8,128)(2,1)} %get-tuple-element.659) | copy-start | bytes 393220 | tf_op jit(solution)/shard_map/while
  255.4 3.2 %copy-start.2 = (f32[2,128,1,16,64]{1,4,3,2,0:T(8,128)S(1)}, f32[2,128,1,16,64]{1,4,3,2,0:T(8,128)}, u32[]{:S(2)}) copy-start(f32[2,128,1,16,64]{1,4,3,2,0:T(8,128)} %get-tuple-element.644) | copy-start | bytes 3145732 | tf_op jit(solution)/shard_map/while
  255.4 3.3 %copy-start.6 = (bf16[2,128,1,16,64]{1,4,3,2,0:T(8,128)(2,1)S(1)}, bf16[2,128,1,16,64]{1,4,3,2,0:T(8,128)(2,1)}, u32[]{:S(2)}) copy-start(bf16[2,128,1,16,64]{1,4,3,2,0:T(8,128)(2,1)} %get-tuple-element.657) | copy-start | bytes 1572868 | tf_op jit(solution)/shard_map/while
  259.2 1.0 copy-start.3
  263.3 3.3 %copy-start.7 = (bf16[2,128,1,256]{3,1,2,0:T(8,128)(2,1)S(1)}, bf16[2,128,1,256]{3,1,2,0:T(8,128)(2,1)}, u32[]{:S(2)}) copy-start(bf16[2,128,1,256]{3,1,2,0:T(8,128)(2,1)} %get-tuple-element.659) | copy-start | bytes 393220 | tf_op jit(solution)/shard_map/while
  263.5 3.2 %copy-start.2 = (f32[2,128,1,16,64]{1,4,3,2,0:T(8,128)S(1)}, f32[2,128,1,16,64]{1,4,3,2,0:T(8,128)}, u32[]{:S(2)}) copy-start(f32[2,128,1,16,64]{1,4,3,2,0:T(8,128)} %get-tuple-element.644) | copy-start | bytes 3145732 | tf_op jit(solution)/shard_map/while
  263.5 3.2 %copy-start.6 = (bf16[2,128,1,16,64]{1,4,3,2,0:T(8,128)(2,1)S(1)}, bf16[2,128,1,16,64]{1,4,3,2,0:T(8,128)(2,1)}, u32[]{:S(2)}) copy-start(bf16[2,128,1,16,64]{1,4,3,2,0:T(8,128)(2,1)} %get-tuple-element.657) | copy-start | bytes 1572868 | tf_op jit(solution)/shard_map/while
  267.3 1.0 copy-start.3
  268.3 2.1 copy-start.1
  270.5 3.1 %copy-start.13 = (f32[16,1,256]{2,1,0:T(1,128)S(1)}, f32[16,1,256]{2,1,0:T(1,128)}, u32[]{:S(2)}) copy-start(f32[16,1,256]{2,1,0:T(1,128)} %get-tuple-element.436) | copy-start | bytes 49156
  275.0 2.3 copy-start.5
  279.1 2.3 copy-start.5
  282.2 1.2 copy-start.4
  282.2 1.5 copy-start.11
  282.2 1.9 copy-start.10
  284.5 2.5 copy-start.8
  284.5 2.5 copy-start.15
  284.5 2.5 copy-start.16
  284.5 2.4 collective-permute-start.2
Sparse Core Ops, SparseCore 0:
  27.7 58.3 all-gather.13
  108.7 54.4 all-gather.15
  169.4 74.0 all-gather.17
